TPU v7x, 512 devices: a whole 4x4x16 slice. The times are simulated.
512 devices in a mesh: row: 16 (over y, z_hi), col: 32 (over z_lo, x, core).
Axes of the slice: x: 4, y: 4, z: 16 (z_hi: 4, z_lo: 4; z = z_hi * 4 + z_lo), core: 2. Of those that a mesh axis runs over, the one named last changes fastest.
Arguments:
- queries: bfloat16 [16384, 768], P(('row', 'col')), may hold values from -8 to 8
- tools: bfloat16 [24576, 768], P(('col', 'row')), may hold values from -8 to 8
- query_mass: float32 [16384], P('row'), may hold values from 0.5 to 5
- tool_mass: float32 [24576], P('col'), may hold values from 0.5 to 5
Outputs:
- mapped_queries: bfloat16 [16384, 768], P(('row', 'col'))
- query_potential: float32 [16384], P('row')
- tool_potential: float32 [24576], P('col')
All inputs are finite; a program needn't handle non-finite values.
Results may differ from a plain program's by a relative error of at most 0.0025.
Values may be sent and summed in bfloat16 or wider, within the bound.
A program may use at most 64 MiB of HBM per device.

v0:
```python
import math

import jax
import jax.numpy as jnp
from jax import lax
from jax.sharding import PartitionSpec as P

ITERS = 3


EPSILON = 0.5


def row_lse(scores):
    local_max = jnp.max(scores, axis=1)
    highest = lax.pmax(local_max, "col")
    summed = lax.psum(jnp.sum(jnp.exp(scores - highest[:, None]), axis=1), "col")
    return highest + jnp.log(summed)


def column_lse(scores):
    local_max = jnp.max(scores, axis=0)
    highest = lax.pmax(local_max, "row")
    summed = lax.psum(jnp.sum(jnp.exp(scores - highest[None, :]), axis=0), "row")
    return highest + jnp.log(summed)


def local(queries, tools, query_mass, tool_mass):
    tool_block = lax.all_gather(tools, "row", axis=0, tiled=True)
    features = queries.shape[1]
    scaling = -1.0 / math.sqrt(features)
    products = lax.dot_general(
        lax.all_gather(queries, "col", axis=0, tiled=True),
        tool_block,
        (((1,), (1,)), ((), ())),
        preferred_element_type=jnp.float32,
    )
    cost_tile = products * scaling
    log_query = jnp.log(query_mass)
    log_tool = jnp.log(tool_mass)
    tool_potential = jnp.zeros((cost_tile.shape[1],), jnp.float32)
    query_potential = jnp.zeros((cost_tile.shape[0],), jnp.float32)
    for sweep in range(ITERS):
        query_potential = EPSILON * log_query - EPSILON * row_lse(
            (tool_potential[None, :] - cost_tile) / EPSILON
        )
        tool_potential = EPSILON * log_tool - EPSILON * column_lse(
            (query_potential[:, None] - cost_tile) / EPSILON
        )
    final_scores = (tool_potential[None, :] - cost_tile) / EPSILON
    peaks = lax.pmax(jnp.max(final_scores, axis=1), "col")
    exps = jnp.exp(final_scores - peaks[:, None])
    local_total = jnp.sum(exps, axis=1)
    weights = exps.astype(jnp.bfloat16)
    own_rows = cost_tile.shape[0] // lax.axis_size("col")
    totals = lax.psum(local_total, "col")
    own_totals = lax.dynamic_slice_in_dim(totals, lax.axis_index("col") * own_rows, own_rows, 0)
    summed = lax.psum_scatter(
        jnp.dot(weights, tool_block, preferred_element_type=jnp.float32),
        "col",
        scatter_dimension=0,
        tiled=True,
    )
    mapped_queries = (summed / own_totals[:, None]).astype(jnp.bfloat16)
    return (mapped_queries, query_potential, tool_potential)


def solution(mesh):
    in_specs = (P(("row", "col"), None), P(("col", "row"), None), P("row"), P("col"))
    out_specs = (P(("row", "col"), None), P("row"), P("col"))
    return jax.shard_map(local, mesh=mesh, in_specs=in_specs, out_specs=out_specs, check_vma=False)
```

profile of v0, /device:TPU:1, one launch (start us, length us, event | category | flops | bytes accessed | tf_op | source)
XLA Modules:
  0.0 1092.2 jit_solution(7041131550528066276)
XLA Ops:
  7.2 0.0 all-gather.5.cloned.1.call-start
  7.2 0.7 all-gather.5.cloned.1.call-update
  7.9 0.0 all-gather.3.cloned.1.call-start
  7.9 0.7 all-gather.3.cloned.1.call-update
  8.6 0.0 reduce-scatter.2.cloned.1.call-start
  8.7 87.1 %all-gather.5.cloned.1.call-done = bf16[768,768]{1,0:T(8,128)(2,1)} async-done(((bf16[48,768]{1,0:T(8,128)(2,1)}), bf16[768,768]{1,0:T(8,128)(2,1)}) %all-gather.5.cloned.1.call-update) | async-done | bytes 1179664 | tf_op jit(solution)/shard_map/all_gather | solution.py:29
  95.8 62.0 %all-gather.3.cloned.1.call-done = bf16[1024,768]{1,0:T(8,128)(2,1)} async-done(((bf16[32,768]{1,0:T(8,128)(2,1)}), bf16[1024,768]{1,0:T(8,128)(2,1)}) %all-gather.3.cloned.1.call-update) | async-done | bytes 1572880 | tf_op jit(solution)/shard_map/all_gather | solution.py:33
  157.9 3.2 fusion
  161.1 0.0 copy-start.2
  161.1 67.0 %pmax.49 = f32[1024]{0:T(1024)S(1)} all-reduce(f32[1024]{0:T(1024)S(1)} %get-tuple-element.3), channel_id=1, replica_groups=mesh['row'=16,'col'=32] {'col'}, use_global_device_ids=true, to_apply=%region_1.0 | all-reduce | flops 1024 | bytes 8192 | tf_op jit(solution)/shard_map/pmax | solution.py:16
  228.1 0.6 exponential_reduce_fusion.5
  228.7 70.2 %psum.49 = f32[1024]{0:T(1024)S(1)} all-reduce(f32[1024]{0:T(1024)S(1)} %exponential_reduce_fusion.5), channel_id=1, replica_groups=mesh['row'=16,'col'=32] {'col'}, use_global_device_ids=true, to_apply=%region_3.0 | all-reduce | flops 1024 | bytes 8192 | tf_op jit(solution)/shard_map/psum | solution.py:17
  298.9 0.0 copy-done.2
  298.9 0.0 copy-start.3
  299.0 0.4 fusion.1
  299.3 46.5 %pmax.50 = f32[768]{0:T(1024)S(1)} all-reduce(f32[768]{0:T(1024)S(1)} %fusion.1), channel_id=1, replica_groups=mesh['row'=16,'col'=32] {'row'}, use_global_device_ids=true, to_apply=%region_5.0 | all-reduce | flops 768 | bytes 6144 | tf_op jit(solution)/shard_map/pmax | solution.py:23
  345.9 0.8 exponential_reduce_fusion.4
  346.7 41.6 %psum.50 = f32[768]{0:T(1024)S(1)} all-reduce(f32[768]{0:T(1024)S(1)} %exponential_reduce_fusion.4), channel_id=1, replica_groups=mesh['row'=16,'col'=32] {'row'}, use_global_device_ids=true, to_apply=%region_7.0 | all-reduce | flops 768 | bytes 6144 | tf_op jit(solution)/shard_map/psum | solution.py:24
  388.3 0.0 copy-done.3
  388.3 0.4 fusion.2
  388.7 81.8 %pmax.51 = f32[1024]{0:T(1024)S(1)} all-reduce(f32[1024]{0:T(1024)S(1)} %fusion.2), channel_id=1, replica_groups=mesh['row'=16,'col'=32] {'col'}, use_global_device_ids=true, to_apply=%region_9.0 | all-reduce | flops 1024 | bytes 8192 | tf_op jit(solution)/shard_map/pmax | solution.py:16
  470.5 0.7 exponential_reduce_fusion.3
  471.2 67.4 %psum.51 = f32[1024]{0:T(1024)S(1)} all-reduce(f32[1024]{0:T(1024)S(1)} %exponential_reduce_fusion.3), channel_id=1, replica_groups=mesh['row'=16,'col'=32] {'col'}, use_global_device_ids=true, to_apply=%region_11.0 | all-reduce | flops 1024 | bytes 8192 | tf_op jit(solution)/shard_map/psum | solution.py:17
  538.6 0.4 fusion.3
  539.0 42.3 %pmax.52 = f32[768]{0:T(1024)S(1)} all-reduce(f32[768]{0:T(1024)S(1)} %fusion.3), channel_id=1, replica_groups=mesh['row'=16,'col'=32] {'row'}, use_global_device_ids=true, to_apply=%region_13.0 | all-reduce | flops 768 | bytes 6144 | tf_op jit(solution)/shard_map/pmax | solution.py:23
  581.4 0.8 exponential_reduce_fusion.2
  582.2 41.7 %psum.52 = f32[768]{0:T(1024)S(1)} all-reduce(f32[768]{0:T(1024)S(1)} %exponential_reduce_fusion.2), channel_id=1, replica_groups=mesh['row'=16,'col'=32] {'row'}, use_global_device_ids=true, to_apply=%region_15.0 | all-reduce | flops 768 | bytes 6144 | tf_op jit(solution)/shard_map/psum | solution.py:24
  623.9 0.4 fusion.4
  624.3 81.8 %pmax.53 = f32[1024]{0:T(1024)S(1)} all-reduce(f32[1024]{0:T(1024)S(1)} %fusion.4), channel_id=1, replica_groups=mesh['row'=16,'col'=32] {'col'}, use_global_device_ids=true, to_apply=%region_17.0 | all-reduce | flops 1024 | bytes 8192 | tf_op jit(solution)/shard_map/pmax | solution.py:16
  706.1 0.7 exponential_reduce_fusion.1
  706.8 67.4 %psum.53 = f32[1024]{0:T(1024)S(1)} all-reduce(f32[1024]{0:T(1024)S(1)} %exponential_reduce_fusion.1), channel_id=1, replica_groups=mesh['row'=16,'col'=32] {'col'}, use_global_device_ids=true, to_apply=%region_19.0 | all-reduce | flops 1024 | bytes 8192 | tf_op jit(solution)/shard_map/psum | solution.py:17
  774.2 0.0 copy-start
  774.2 0.4 fusion.5
  774.6 42.3 %pmax.54 = f32[768]{0:T(1024)S(1)} all-reduce(f32[768]{0:T(1024)S(1)} %fusion.5), channel_id=1, replica_groups=mesh['row'=16,'col'=32] {'row'}, use_global_device_ids=true, to_apply=%region_21.0 | all-reduce | flops 768 | bytes 6144 | tf_op jit(solution)/shard_map/pmax | solution.py:23
  816.8 0.8 exponential_reduce_fusion
  817.6 0.0 copy-done
  817.6 41.7 %psum.54 = f32[768]{0:T(1024)S(1)} all-reduce(f32[768]{0:T(1024)S(1)} %exponential_reduce_fusion), channel_id=1, replica_groups=mesh['row'=16,'col'=32] {'row'}, use_global_device_ids=true, to_apply=%region_23.0 | all-reduce | flops 768 | bytes 6144 | tf_op jit(solution)/shard_map/psum | solution.py:24
  859.4 0.0 copy-start.1
  859.4 0.4 fusion.6
  859.8 81.8 %pmax.55 = f32[1024]{0:T(1024)S(1)} all-reduce(f32[1024]{0:T(1024)S(1)} %fusion.6), channel_id=1, replica_groups=mesh['row'=16,'col'=32] {'col'}, use_global_device_ids=true, to_apply=%region_25.0 | all-reduce | flops 1024 | bytes 8192 | tf_op jit(solution)/shard_map/pmax | solution.py:51
  941.6 4.5 fusion.9
  946.1 0.0 reduce-scatter.2.cloned.1.call-update
  946.2 0.0 copy-done.1
  946.2 0.7 fusion.7
  946.9 67.4 %psum.55 = f32[1024]{0:T(1024)S(1)} all-reduce(f32[1024]{0:T(1024)S(1)} %fusion.7), channel_id=1, replica_groups=mesh['row'=16,'col'=32] {'col'}, use_global_device_ids=true, to_apply=%region_28.0 | all-reduce | flops 1024 | bytes 8192 | tf_op jit(solution)/shard_map/psum | solution.py:56
  1014.3 0.1 dynamic_slice.3
  1014.4 69.7 %reduce-scatter.2.cloned.1.call-done = f32[32,768]{1,0:T(8,128)} async-done(((f32[1024,768]{1,0:T(8,128)}), f32[32,768]{1,0:T(8,128)}) %reduce-scatter.2.cloned.1.call-update) | async-done | bytes 98320 | tf_op jit(solution)/shard_map/reduce_scatter | solution.py:58
  1084.0 1.6 divide_convert_fusion
  (6 shorter events, 0.1 us)
Async XLA Ops:
  7.2 88.7 %all-gather.5.cloned.1.call-start = ((), (), s32[]{:S(2)}) async-start(), calls=%async_computation.2 | async-start | bytes 1253376 | tf_op jit(solution)/shard_map/all_gather | solution.py:29
  7.9 150.0 %all-gather.3.cloned.1.call-start = ((), (), s32[]{:S(2)}) async-start(), calls=%async_computation.1 | async-start | bytes 1622016 | tf_op jit(solution)/shard_map/all_gather | solution.py:33
  8.6 1075.4 %reduce-scatter.2.cloned.1.call-start = ((), (), s32[]{:S(2)}) async-start(), calls=%async_computation.3 | async-start | bytes 3244032 | tf_op jit(solution)/shard_map/reduce_scatter | solution.py:58
  161.1 137.9 %copy-start.2 = (f32[1024]{0:T(1024)S(1)}, f32[1024]{0:T(1024)}, u32[]{:S(2)}) copy-start(f32[1024]{0:T(1024)} %param.6) | copy-start | bytes 12292
  298.9 89.4 %copy-start.3 = (f32[768]{0:T(1024)S(1)}, f32[768]{0:T(1024)}, u32[]{:S(2)}) copy-start(f32[768]{0:T(1024)} %param.7) | copy-start | bytes 9220
  774.2 43.5 %copy-start = (f32[1024]{0:T(1024)}, f32[1024]{0:T(1024)S(1)}, u32[]{:S(2)}) copy-start(f32[1024]{0:T(1024)S(1)} %multiply_subtract_fusion.1) | copy-start | bytes 12292
  859.4 86.8 %copy-start.1 = (f32[768]{0:T(1024)}, f32[768]{0:T(1024)S(1)}, u32[]{:S(2)}) copy-start(f32[768]{0:T(1024)S(1)} %multiply_subtract_fusion) | copy-start | bytes 9220
Sparse Core Ops, SparseCore 0:
  11.1 84.7 all-gather.4
  98.0 59.8 all-gather.2
  946.3 137.7 reduce-scatter.1
where the time goes:
time: 1100 us; the launch traced here: 1090 us
  blocking collectives  841 us (76%)
  waiting for transfers between devices  220 us (20%)
  between operations  13.9 us (1%)
    pmax x3, blocking collectives, row_lse(): highest = lax.pmax(local_max, 'col')  231 us
    psum x3, blocking collectives, row_lse(): lax.psum(jnp.sum(jnp.exp(scores - highest[:, None]), axis=1), 'col')  205 us
    pmax x3, blocking collectives, column_lse(): highest = lax.pmax(local_max, 'row')  131 us
    psum x3, blocking collectives, column_lse(): lax.psum(jnp.sum(jnp.exp(scores - highest[None, :]), axis=0), 'row')  125 us
    all_gather x1, waiting for transfers between devices, local(): tool_block = lax.all_gather(tools, 'row', axis=0, tiled=True)  87.1 us
    pmax x1, blocking collectives, local(): peaks = lax.pmax(jnp.max(final_scores, axis=1), 'col')  81.8 us
    reduce_scatter x1, waiting for transfers between devices, local(): lax.psum_scatter(jnp.dot(weights, tool_block, preferred_element_type=jnp....  69.7 us
    psum x1, blocking collectives, local(): totals = lax.psum(local_total, 'col')  67.4 us
  transfers between devices with their start and end apart: 3, of which 3 were waited for; matrix products, arithmetic and copies ran while one was open for 0% of the time, Pallas kernels for 0%

commit v1 on v0

v1 whole, which is shorter than its diff:
```python
import math

import jax
import jax.numpy as jnp
from jax import lax
from jax.experimental import pallas as pl
from jax.experimental.pallas import tpu as pltpu
from jax.sharding import PartitionSpec as P

MESH = pl.DeviceIdType.MESH
EPSILON = 0.5
F32 = jnp.float32
BF16 = jnp.bfloat16
NX, NY, NL, NH = 4, 4, 4, 4
NZ = NL * NH
CHIPS = NX * NY
D = 768
QS, TS = 32, 48
QB, TB = 2 * CHIPS * QS, NZ * TS
LOG2E = 1.4426950408889634
POT = EPSILON / LOG2E


def kernel(
    q_ref, t_ref, qm_ref, tm_ref,
    map_ref, qp_ref, tp_ref,
    qblk, tblk, tsib, plan, w, wsib, part, got, cols,
    rsend, rbuf, csend, cbuf, qmb, tms, tmb, fout, qpb, gout, tpb,
    q_send, q_recv, q_fwd, q_sib, t_send, t_recv, s_send, s_recv, ws_send, ws_recv,
    m_send, m_recv, r_send, r_recv, c_send, c_recv, o_send, o_recv, p_send, p_recv,
):
    row, col = lax.axis_index("row"), lax.axis_index("col")
    y, zh = row // NH, row % NH
    zl, x, core = col // (2 * NX), (col // 2) % NX, col % 2
    z = zh * NL + zl
    sib = 1 - core
    chip = y * NX + x
    mine = chip * 2 + core
    slot = zl * NH + zh

    def device(x_, y_, z_, core_):
        return (y_ * NH + z_ // NL, ((z_ % NL) * NX + x_) * 2 + core_)

    def group_peer(j):
        y_ = (y + j // (2 * NX)) % NY
        x_ = (x + (j // 2) % NX) % NX
        return device(x_, y_, z, (core + j) % 2)

    def chip_peer(j):
        return (x + j % NX) % NX, (y + j // NX) % NY

    def z_peer(j):
        return device(x, y, (z + j) % NZ, core)

    def send(src, dst, s_sem, r_sem, dev):
        pltpu.make_async_remote_copy(
            src_ref=src, dst_ref=dst, send_sem=s_sem, recv_sem=r_sem, device_id=dev, device_id_type=MESH
        ).start()

    def wait(ref, sem):
        pltpu.make_async_copy(ref, ref, sem).wait()

    barrier = pltpu.get_barrier_semaphore()

    @pl.loop(1, 2 * CHIPS)
    def _(j):
        pl.semaphore_signal(barrier, inc=1, device_id=group_peer(j), device_id_type=MESH)

    @pl.loop(1, NZ)
    def _(j):
        pl.semaphore_signal(barrier, inc=1, device_id=z_peer(j), device_id_type=MESH)

    tms_all = tm_ref[...]
    for i in range(NY):
        tms[i] = tms_all[:, i * NH * TS:(i + 1) * NH * TS]
    pl.semaphore_wait(barrier, 2 * CHIPS - 1 + NZ - 1)

    right, left = device(x, y, (z + 1) % NZ, core), device(x, y, (z + NZ - 1) % NZ, core)

    def t_slot(z_):
        return (z_ % NL) * NH + z_ // NL

    def t_copy(way, step, source):
        s = t_slot(source)
        src = t_ref if step == 0 else tblk.at[s]
        send(src, tblk.at[s], t_send.at[way], t_recv.at[way, step], right if way == 0 else left)

    t_copy(0, 0, z)
    t_copy(1, 0, z)

    @pl.loop(1, CHIPS)
    def _(j):
        x_, y_ = chip_peer(j)
        send(q_ref, qblk.at[mine], q_send, q_recv.at[chip], device(x_, y_, z, core))

    send(q_ref, qblk.at[mine], q_fwd, q_sib, device(x, y, z, sib))
    for j in range(1, NY):
        send(qm_ref.at[zl], qmb.at[y], m_send.at[0], m_recv.at[0], device(x, (y + j) % NY, z, core))
    for j in range(1, NL):
        send(tms.at[y], tmb.at[zl], m_send.at[1], m_recv.at[1], device(x, y, zh * NL + (zl + j) % NL, core))
    qblk[mine] = q_ref[...]
    tblk[slot] = t_ref[...]
    qmb[y] = qm_ref[zl]
    tmb[zl] = tms[y]

    STEPS = (NZ // 2, NZ // 2 - 1)
    for step in range(NZ // 2):
        for way in (0, 1):
            if step < STEPS[way]:
                source = (z - 1 - step + NZ) % NZ if way == 0 else (z + 1 + step) % NZ
                wait(tblk.at[t_slot(source)], t_recv.at[way, step])
                if step + 1 < STEPS[way]:
                    t_copy(way, step + 1, source)
        for j in range(1 + 2 * step, min(3 + 2 * step, CHIPS)):
            x_, y_ = (x + NX - j % NX) % NX, (y + NY - j // NX) % NY
            chip_ = y_ * NX + x_
            s = chip_ * 2 + core
            wait(qblk.at[s], q_recv.at[chip_])
            send(qblk.at[s], qblk.at[s], q_fwd, q_sib, device(x, y, z, sib))
    send(tblk, tsib, s_send, s_recv, device(x, y, z, sib))
    wait(qblk.at[pl.ds(0, CHIPS)], q_sib)

    wait(qmb.at[pl.ds(0, NY - 1)], m_recv.at[0])
    wait(tmb.at[pl.ds(0, NL - 1)], m_recv.at[1])
    lane = lax.broadcasted_iota(jnp.int32, (8, 128), 1)
    sub = lax.broadcasted_iota(jnp.int32, (8, 128), 0)
    mass_q = jnp.zeros((8, 128), F32)
    for b in range(8):
        line = qmb[b // 2, pl.ds(b % 2, 1), :]
        spread = jnp.broadcast_to(line, (128, 128)).T
        for k in range(16):
            mass_q = jnp.where(lane == b * 16 + k, spread[k * 8:k * 8 + 8, :], mass_q)
    mass_t = jnp.concatenate([tmb[i] for i in range(NL)], axis=1)

    def dense(v):
        out = jnp.zeros((8, 128), F32)
        for c in range(TB // 128):
            out = jnp.where(sub == c, v[:, c * 128:(c + 1) * 128], out)
        return out

    def undense(v):
        return jnp.concatenate([v[c:c + 1, :] for c in range(TB // 128)], axis=1)

    def gather_rows(n, value):
        rsend[n] = value
        rbuf[n, mine] = value

        @pl.loop(1, 2 * CHIPS)
        def _(j):
            send(rsend.at[n], rbuf.at[n, mine], r_send.at[n], r_recv.at[n], group_peer(j))

    def wait_rows(n):
        wait(rbuf.at[n, pl.ds(0, 2 * CHIPS - 1)], r_recv.at[n])
        return rbuf[n]

    def gather_cols(n, value):
        csend[n] = value
        cbuf[n, z] = value

        @pl.loop(1, NZ)
        def _(j):
            send(csend.at[n], cbuf.at[n, z], c_send.at[n], c_recv.at[n], z_peer(j))

    def wait_cols(n):
        wait(cbuf.at[n, pl.ds(0, NZ - 1)], c_recv.at[n])
        return cbuf[n]

    def lse(parts):
        top = jnp.max(parts, axis=0)
        return top + jnp.log2(jnp.sum(jnp.exp2(parts - top[None]), axis=0))

    RB = 64
    NB = QB // RB

    def pick(out, block, values):
        for g in range(RB // 8):
            out = jnp.where(lane == block * (RB // 8) + g, values[g * 8:(g + 1) * 8, :], out)
        return out

    def spread_rows(value):
        def body(b, v):
            for k in range(16):
                cols[pl.ds(pl.multiple_of(b * 128 + k * 8, 8), 8), :] = jnp.broadcast_to(v[:, k:k + 1], (8, 128))
            return pltpu.roll(v, 112, 1)
        lax.fori_loop(0, 8, body, value)

    def wide(r0, rows):
        return jnp.concatenate([cols[pl.ds(r0, rows), :]] * (TB // 128), axis=1)

    zero = jnp.zeros((8, 128), F32)

    scale = LOG2E / (EPSILON * math.sqrt(D))
    tools = tblk[...].reshape(TB, D)
    MB = 256

    def products(i, carry):
        a = qblk[pl.ds(i * (MB // QS), MB // QS)].reshape(MB, D)
        s = lax.dot_general(a, tools, (((1,), (1,)), ((), ())), preferred_element_type=F32)
        plan[pl.ds(pl.multiple_of(i * MB, MB), MB), :] = s * scale
        return carry

    lax.fori_loop(0, QB // MB, products, 0)

    def first_rows(i, carry):
        tops, sums = carry
        s = plan[pl.ds(pl.multiple_of(i * RB, RB), RB), :]
        top = jnp.max(s, axis=1, keepdims=True)
        total = jnp.sum(jnp.exp2(s - top), axis=1, keepdims=True)
        return pick(tops, i, top), pick(sums, i, total)

    tops, sums = lax.fori_loop(0, NB, first_rows, (zero, zero))
    gather_rows(0, tops + jnp.log2(sums))
    first_f = jnp.log2(mass_q) - lse(wait_rows(0))

    spread_rows(first_f)

    def col_max(i, top):
        r0 = pl.multiple_of(i * RB, RB)
        s = plan[pl.ds(r0, RB), :] + wide(r0, RB)
        plan[pl.ds(r0, RB), :] = s
        return jnp.maximum(top, jnp.max(s.reshape(RB // 8, 8, TB), axis=0))

    top8 = lax.fori_loop(0, NB, col_max, jnp.full((8, TB), -jnp.inf, F32))
    top = jnp.max(top8, axis=0, keepdims=True)

    def col_sum(i, acc):
        s = plan[pl.ds(pl.multiple_of(i * RB, RB), RB), :]
        return acc + jnp.sum(jnp.exp2(s - top).reshape(RB // 8, 8, TB), axis=0)

    acc = lax.fori_loop(0, NB, col_sum, jnp.zeros((8, TB), F32))
    gather_cols(0, dense(top + jnp.log2(jnp.sum(acc, axis=0, keepdims=True))))
    first_g = jnp.log2(mass_t) - undense(lse(wait_cols(0)))

    def second_rows(i, sums):
        r0 = pl.multiple_of(i * RB, RB)
        e = jnp.exp2(plan[pl.ds(r0, RB), :] + first_g)
        plan[pl.ds(r0, RB), :] = e
        return pick(sums, i, jnp.sum(e, axis=1, keepdims=True))

    def later_rows(v):
        def body(i, sums):
            e = plan[pl.ds(pl.multiple_of(i * RB, RB), RB), :] * v
            return pick(sums, i, jnp.sum(e, axis=1, keepdims=True))
        return lax.fori_loop(0, NB, body, zero)

    def later_cols():
        def body(i, acc):
            r0 = pl.multiple_of(i * RB, RB)
            e = plan[pl.ds(r0, RB), :] * wide(r0, RB)
            return acc + jnp.sum(e.reshape(RB // 8, 8, TB), axis=0)
        acc = lax.fori_loop(0, NB, body, jnp.zeros((8, TB), F32))
        return dense(jnp.sum(acc, axis=0, keepdims=True))

    gather_rows(1, lax.fori_loop(0, NB, second_rows, zero))
    u = mass_q / jnp.sum(wait_rows(1), axis=0)
    spread_rows(u)
    gather_cols(1, later_cols())
    v = mass_t / undense(jnp.sum(wait_cols(1), axis=0))
    gather_rows(2, later_rows(v))
    u = mass_q / jnp.sum(wait_rows(2), axis=0)
    spread_rows(u)
    gather_cols(2, later_cols())

    f = (first_f + jnp.log2(u)) * POT
    for b in range(8):
        block = jnp.concatenate(
            [jnp.broadcast_to(f[:, b * 16 + k:b * 16 + k + 1], (8, 128)) for k in range(16)], axis=0
        )
        fout[b // 2, pl.ds(b % 2, 1), :] = block.T[0:1, :]
    for j in range(1, NL):
        send(fout.at[y], qpb.at[zl], o_send.at[0], o_recv.at[0], device(x, y, zh * NL + (zl + j) % NL, core))
    qpb[zl] = fout[y]
    v = mass_t / undense(jnp.sum(wait_cols(2), axis=0))

    PB = 2 * QS

    def weights(i, sums):
        c = ((y + 1 + i // NX) % NY) * NX + i % NX
        r0 = pl.multiple_of(c * PB, PB)
        e = (plan[pl.ds(r0, PB), :] * wide(r0, PB) * v).astype(BF16)
        w[c] = e.reshape(2, QS, TB)
        return pick(sums, c, jnp.sum(e.astype(F32), axis=1, keepdims=True))

    wait(tsib, s_recv)
    sums = zero
    for h in range(NY):
        sums = lax.fori_loop(h * NX, (h + 1) * NX, weights, sums)
        y_ = (y + 1 + h) % NY
        send(w.at[pl.ds(y_ * NX, NX), sib], wsib.at[pl.ds(y_ * NX, NX)], ws_send, ws_recv.at[h], device(x, y, z, sib))
    gather_rows(3, sums)

    own, other = tools, tsib[...].reshape(TB, D)
    for h in range(NY):
        y_ = (y + 1 + h) % NY
        a = w[pl.ds(y_ * NX, NX), core].reshape(NX * QS, TB)
        p = jnp.dot(a, own, preferred_element_type=F32)
        wait(wsib.at[pl.ds(y_ * NX, NX)], ws_recv.at[h])
        b = wsib[pl.ds(y_ * NX, NX)].reshape(NX * QS, TB)
        p = p + jnp.dot(b, other, preferred_element_type=F32)
        part[pl.ds(y_ * NX, NX)] = p.reshape(NX, QS, D)
        for j in range(NX):
            x_ = (x + 1 + j) % NX
            if h < NY - 1 or j < NX - 1:
                send(part.at[y_ * NX + x_], got.at[chip], p_send, p_recv, device(x_, y_, z, core))

    g = (first_g + jnp.log2(v)) * POT
    for i in range(NL):
        gout[i] = g[:, i * NH * TS:(i + 1) * NH * TS]
    for j in range(1, NY):
        send(gout.at[zl], tpb.at[y], o_send.at[1], o_recv.at[1], device(x, (y + j) % NY, z, core))
    tpb[y] = gout[zl]
    wait(qpb.at[pl.ds(0, NL - 1)], o_recv.at[0])
    wait(tpb.at[pl.ds(0, NY - 1)], o_recv.at[1])
    qp_ref[...] = qpb[...]
    tp_ref[...] = jnp.concatenate([tpb[i] for i in range(NY)], axis=1)

    totals = jnp.sum(wait_rows(3), axis=0)
    spread_rows(totals)
    total = cols[pl.ds(pl.multiple_of(mine * QS, QS), QS), :]
    got[chip] = part[chip]
    wait(got.at[pl.ds(0, CHIPS - 1)], p_recv)
    full = jnp.sum(got[...], axis=0)
    map_ref[...] = (full / jnp.concatenate([total] * (D // 128), axis=1)).astype(BF16)

    wait(qblk.at[pl.ds(0, CHIPS - 1)], q_send)
    wait(qblk.at[pl.ds(0, CHIPS)], q_fwd)
    for way in (0, 1):
        wait(tblk.at[pl.ds(0, STEPS[way])], t_send.at[way])
    wait(tblk, s_send)
    wait(wsib, ws_send)
    wait(qmb.at[pl.ds(0, NY - 1)], m_send.at[0])
    wait(tmb.at[pl.ds(0, NL - 1)], m_send.at[1])
    wait(qpb.at[pl.ds(0, NL - 1)], o_send.at[0])
    wait(tpb.at[pl.ds(0, NY - 1)], o_send.at[1])
    for n in range(4):
        wait(rbuf.at[n, pl.ds(0, 2 * CHIPS - 1)], r_send.at[n])
    for n in range(3):
        wait(cbuf.at[n, pl.ds(0, NZ - 1)], c_send.at[n])
    wait(got.at[pl.ds(0, CHIPS - 1)], p_send)


def local(queries, tools, query_mass, tool_mass):
    vmem = pl.BlockSpec(memory_space=pltpu.VMEM)
    dma, V = pltpu.SemaphoreType.DMA, pltpu.VMEM
    mapped, qp, tp = pl.pallas_call(
        kernel,
        out_shape=(
            jax.ShapeDtypeStruct((QS, D), BF16),
            jax.ShapeDtypeStruct((NL, 2, 128), F32),
            jax.ShapeDtypeStruct((1, TB), F32),
        ),
        in_specs=[vmem] * 4,
        out_specs=(vmem,) * 3,
        scratch_shapes=[
            V((2 * CHIPS, QS, D), BF16), V((NZ, TS, D), BF16), V((NZ, TS, D), BF16), V((QB, TB), F32),
            V((CHIPS, 2, QS, TB), BF16), V((CHIPS, QS, TB), BF16), V((CHIPS, QS, D), F32), V((CHIPS, QS, D), F32),
            V((QB, 128), F32),
            V((4, 8, 128), F32), V((4, 2 * CHIPS, 8, 128), F32), V((3, 8, 128), F32), V((3, NZ, 8, 128), F32),
            V((NY, 2, 128), F32), V((NY, 1, NH * TS), F32), V((NL, 1, NH * TS), F32),
            V((NY, 2, 128), F32), V((NL, 2, 128), F32), V((NL, 1, NH * TS), F32), V((NY, 1, NH * TS), F32),
            dma, dma((CHIPS,)), dma, dma, dma((2,)), dma((2, NZ // 2)), dma, dma, dma, dma((NY,)),
            dma((2,)), dma((2,)), dma((4,)), dma((4,)), dma((3,)), dma((3,)), dma((2,)), dma((2,)), dma, dma,
        ],
        compiler_params=pltpu.CompilerParams(
            collective_id=0, has_side_effects=True, vmem_limit_bytes=48 * 1024 * 1024
        ),
    )(queries, tools, query_mass.reshape(NL, 2, 128), tool_mass.reshape(1, TB))
    return mapped, qp.reshape(QB), tp.reshape(TB)


def solution(mesh):
    in_specs = (P(("row", "col"), None), P(("col", "row"), None), P("row"), P("col"))
    out_specs = (P(("row", "col"), None), P("row"), P("col"))
    return jax.shard_map(local, mesh=mesh, in_specs=in_specs, out_specs=out_specs, check_vma=False)
```

time: 1100 us -> 135 us (0.12)
  blocking collectives: 841 us -> 0 us
  waiting for transfers between devices: 220 us -> 0 us
  Pallas kernels: 0 us -> 130 us
  between operations: 13.9 us -> 0.65 us
    pmax x7 -> x0, blocking collectives: 444 us -> none  [the longest x3 231 us: row_lse(): highest = lax.pmax(local_max, 'col')]
    psum x7 -> x0, blocking collectives: 397 us -> none  [the longest x3 205 us: row_lse(): lax.psum(jnp.sum(jnp.exp(scores - highest[:, None]), axis=1), 'col')]
    all_gather x2 -> x0, waiting for transfers between devices: 149 us -> none  [the longest x1 87.1 us: local(): tool_block = lax.all_gather(tools, 'row', axis=0, tiled=True)]
    pallas_call x0 -> x1, Pallas kernels: none -> 130 us  [local(): pl.pallas_call(kernel, out_shape=(jax.ShapeDtypeStruct((QS, D), BF16), ja...]
    reduce_scatter x1 -> x0, waiting for transfers between devices: 69.7 us -> none  [local(): lax.psum_scatter(jnp.dot(weights, tool_block, preferred_element_type=jnp....]
  transfers between devices with their start and end apart: 3 -> 0, of which waited for: 3 -> 0; matrix products, arithmetic and copies ran while one was open for 0% -> 0% of each run, Pallas kernels for 0% -> 0%
where the time goes in v1:
time: 135 us
  Pallas kernels  130 us (96%)
  local copies, waits for them, and re-layouts  3.59 us (3%)
    pallas_call x1, Pallas kernels, local(): pl.pallas_call(kernel, out_shape=(jax.ShapeDtypeStruct((QS, D), BF16), ja...  130 us
    unnamed x8, local copies, waits for them, and re-layouts  2.9 us

profile of v1, /device:TPU:1, one launch (start us, length us, event | category | flops | bytes accessed | tf_op | source)
XLA Modules:
  0.0 134.6 jit_solution(9432471790696803219)
XLA Ops:
  0.6 0.0 copy-start.2
  0.6 0.7 reshape.19.tm_ref
  1.3 0.0 copy-done.2
  1.3 0.0 copy-start
  1.3 0.9 copy-done
  2.2 0.0 copy-start.1
  2.2 0.8 copy-done.1
  3.0 129.8 %shard_map.67 = (bf16[32,768]{1,0:T(8,128)(2,1)S(1)}, f32[4,2,128]{2,1,0:T(2,128)S(1)}, f32[1,768]{1,0:T(1,128)S(1)}) custom-call(bf16[32,768]{1,0:T(8,128)(2,1)S(1)} %copy-done.1, bf16[48,768]{1,0:T(8,128)(2,1)S(1)} %copy-done, f32[4,2,128]{2,1,0:T(2,128)S(1)} %bitcast.2, f32[1,768]{1,0:T(1,128)S(1)} %reshape.19.tm_ref), custom_call_target="tpu_custom_call" | custom-call | tf_op jit(solution)/shard_map/pallas_call | solution.py:345
  132.8 0.6 reduce
  133.4 0.6 copy.9
  134.0 0.6 copy.10
Async XLA Ops:
  0.6 0.7 copy-start.2
  1.3 0.9 copy-start
  2.2 0.8 copy-start.1

commit v2 on v1

--- a/solution.py
+++ b/solution.py
@@ -22,11 +22,11 @@
 
 
 def kernel(
-    q_ref, t_ref, qm_ref, tm_ref,
+    q_hbm, t_hbm, qm_hbm, tm_hbm,
     map_ref, qp_ref, tp_ref,
     qblk, tblk, tsib, plan, w, wsib, part, got, cols,
-    rsend, rbuf, csend, cbuf, qmb, tms, tmb, fout, qpb, gout, tpb,
-    q_send, q_recv, q_fwd, q_sib, t_send, t_recv, s_send, s_recv, ws_send, ws_recv,
+    qm_ref, tm_ref, rsend, rbuf, csend, cbuf, qmb, tms, tmb, fout, qpb, gout, tpb,
+    l_sem, q_send, q_recv, q_fwd, q_sib, t_send, t_recv, s_send, s_recv, ws_send, ws_recv,
     m_send, m_recv, r_send, r_recv, c_send, c_recv, o_send, o_recv, p_send, p_recv,
 ):
     row, col = lax.axis_index("row"), lax.axis_index("col")
@@ -41,16 +41,19 @@
     def device(x_, y_, z_, core_):
         return (y_ * NH + z_ // NL, ((z_ % NL) * NX + x_) * 2 + core_)
 
+    def far(j, n):
+        return (n // 2 + ((j + 1) // 2) * (1 - 2 * (j % 2)) + n) % n
+
     def group_peer(j):
-        y_ = (y + j // (2 * NX)) % NY
-        x_ = (x + (j // 2) % NX) % NX
-        return device(x_, y_, z, (core + j) % 2)
+        y_ = (y + far(j // (2 * NX), NY)) % NY
+        x_ = (x + far((j // 2) % NX, NX)) % NX
+        return device(x_, y_, z, (core + 1 + j) % 2)
 
     def chip_peer(j):
         return (x + j % NX) % NX, (y + j // NX) % NY
 
     def z_peer(j):
-        return device(x, y, (z + j) % NZ, core)
+        return device(x, y, (z + far(j, NZ)) % NZ, core)
 
     def send(src, dst, s_sem, r_sem, dev):
         pltpu.make_async_remote_copy(
@@ -61,69 +64,117 @@
         pltpu.make_async_copy(ref, ref, sem).wait()
 
     barrier = pltpu.get_barrier_semaphore()
-
-    @pl.loop(1, 2 * CHIPS)
+    for near in (2, NZ - 2, 1, NZ - 1):
+        peer = device(x, y, (z + near) % NZ, core)
+        pl.semaphore_signal(barrier, inc=1, device_id=peer, device_id_type=MESH)
+
+    @pl.loop(0, 2 * CHIPS - 1)
     def _(j):
         pl.semaphore_signal(barrier, inc=1, device_id=group_peer(j), device_id_type=MESH)
 
-    @pl.loop(1, NZ)
-    def _(j):
-        pl.semaphore_signal(barrier, inc=1, device_id=z_peer(j), device_id_type=MESH)
-
-    tms_all = tm_ref[...]
+    loads = [
+        pltpu.make_async_copy(t_hbm, tblk.at[slot], l_sem.at[0]),
+        pltpu.make_async_copy(q_hbm, qblk.at[mine], l_sem.at[1]),
+        pltpu.make_async_copy(qm_hbm, qm_ref, l_sem.at[2]),
+        pltpu.make_async_copy(tm_hbm, tm_ref, l_sem.at[3]),
+    ]
+    for load in loads:
+        load.start()
+    for load in loads:
+        load.wait()
+    tms_all = jnp.concatenate([tm_ref[c:c + 1, :] for c in range(TB // 128)], axis=1)
     for i in range(NY):
         tms[i] = tms_all[:, i * NH * TS:(i + 1) * NH * TS]
-    pl.semaphore_wait(barrier, 2 * CHIPS - 1 + NZ - 1)
-
-    right, left = device(x, y, (z + 1) % NZ, core), device(x, y, (z + NZ - 1) % NZ, core)
+    pl.semaphore_wait(barrier, 2 * CHIPS - 1 + 4)
+
+    lane = lax.broadcasted_iota(jnp.int32, (8, 128), 1)
+    zero = jnp.zeros((8, 128), F32)
+    RB = 64
+    NB = QB // RB
+
+    def pick(out, block, values):
+        n = values.shape[0] // 8
+        for g in range(n):
+            out = jnp.where(lane == block * n + g, values[g * 8:(g + 1) * 8, :], out)
+        return out
+
+    scale = LOG2E / (EPSILON * math.sqrt(D))
+    HB, MB = TB // 2, 256
+
+    def products(half):
+        lanes = pl.ds(pl.multiple_of(half * HB, 128), HB)
+        tools = tblk[pl.ds(half * (NZ // 2), NZ // 2)].reshape(HB, D)
+
+        def body(i, carry):
+            tops, sums = carry
+            a = qblk[pl.ds(i * (MB // QS), MB // QS)].reshape(MB, D)
+            s = scale * lax.dot_general(a, tools, (((1,), (1,)), ((), ())), preferred_element_type=F32)
+            plan[pl.ds(pl.multiple_of(i * MB, MB), MB), lanes] = s
+            top = jnp.max(s, axis=1, keepdims=True)
+            total = jnp.sum(jnp.exp2(s - top), axis=1, keepdims=True)
+            return pick(tops, i, top), pick(sums, i, total)
+
+        return lax.fori_loop(0, QB // MB, body, (zero, zero))
 
     def t_slot(z_):
         return (z_ % NL) * NH + z_ // NL
 
-    def t_copy(way, step, source):
-        s = t_slot(source)
-        src = t_ref if step == 0 else tblk.at[s]
-        send(src, tblk.at[s], t_send.at[way], t_recv.at[way, step], right if way == 0 else left)
-
-    t_copy(0, 0, z)
-    t_copy(1, 0, z)
+    PIECES, PIECE = 3, TS // 3
+
+    def t_piece(source, p):
+        return tblk.at[t_slot(source), pl.ds(p * PIECE, PIECE)]
+
+    REACH = (NZ // 2, NZ // 2 - 1)
+
+    def t_source(way, dist):
+        return (z + NZ - dist) % NZ if way == 0 else (z + dist) % NZ
+
+    def t_forward(way, dist, p):
+        piece = t_piece(t_source(way, dist), p)
+        for hop in (2, 1):
+            if dist % 2 == 0 and dist + hop <= REACH[way]:
+                to = device(x, y, t_source(way, NZ - hop), core)
+                send(piece, piece, t_send.at[way], t_recv.at[way, dist + hop - 1, p], to)
+
+    for p in range(PIECES):
+        for way in (0, 1):
+            t_forward(way, 0, p)
 
     @pl.loop(1, CHIPS)
     def _(j):
         x_, y_ = chip_peer(j)
-        send(q_ref, qblk.at[mine], q_send, q_recv.at[chip], device(x_, y_, z, core))
-
-    send(q_ref, qblk.at[mine], q_fwd, q_sib, device(x, y, z, sib))
+        send(qblk.at[mine], qblk.at[mine], q_send, q_recv.at[chip], device(x_, y_, z, core))
+
+    send(qblk.at[mine], qblk.at[mine], q_fwd, q_sib, device(x, y, z, sib))
     for j in range(1, NY):
         send(qm_ref.at[zl], qmb.at[y], m_send.at[0], m_recv.at[0], device(x, (y + j) % NY, z, core))
-    for j in range(1, NL):
-        send(tms.at[y], tmb.at[zl], m_send.at[1], m_recv.at[1], device(x, y, zh * NL + (zl + j) % NL, core))
-    qblk[mine] = q_ref[...]
-    tblk[slot] = t_ref[...]
     qmb[y] = qm_ref[zl]
     tmb[zl] = tms[y]
 
-    STEPS = (NZ // 2, NZ // 2 - 1)
-    for step in range(NZ // 2):
-        for way in (0, 1):
-            if step < STEPS[way]:
-                source = (z - 1 - step + NZ) % NZ if way == 0 else (z + 1 + step) % NZ
-                wait(tblk.at[t_slot(source)], t_recv.at[way, step])
-                if step + 1 < STEPS[way]:
-                    t_copy(way, step + 1, source)
-        for j in range(1 + 2 * step, min(3 + 2 * step, CHIPS)):
+    for step, dist in enumerate((2, 1, 4, 3, 6, 5, 7, 8)):
+        for p in range(PIECES):
+            for way in (0, 1):
+                if dist <= REACH[way]:
+                    wait(t_piece(t_source(way, dist), p), t_recv.at[way, dist - 1, p])
+                    t_forward(way, dist, p)
+        for j in range(1 + 3 * (step - 2), min(4 + 3 * (step - 2), CHIPS)):
+            if j < 1:
+                continue
             x_, y_ = (x + NX - j % NX) % NX, (y + NY - j // NX) % NY
             chip_ = y_ * NX + x_
             s = chip_ * 2 + core
             wait(qblk.at[s], q_recv.at[chip_])
             send(qblk.at[s], qblk.at[s], q_fwd, q_sib, device(x, y, z, sib))
+        if step == NL - 1:
+            for j in range(1, NL):
+                send(tms.at[y], tmb.at[zl], m_send.at[1], m_recv.at[1], device(x, y, zh * NL + (zl + j) % NL, core))
+        if step == NZ // 2 - 2:
+            wait(qblk.at[pl.ds(0, CHIPS)], q_sib)
+            early = products(1 - zl // 2)
     send(tblk, tsib, s_send, s_recv, device(x, y, z, sib))
-    wait(qblk.at[pl.ds(0, CHIPS)], q_sib)
 
     wait(qmb.at[pl.ds(0, NY - 1)], m_recv.at[0])
     wait(tmb.at[pl.ds(0, NL - 1)], m_recv.at[1])
-    lane = lax.broadcasted_iota(jnp.int32, (8, 128), 1)
-    sub = lax.broadcasted_iota(jnp.int32, (8, 128), 0)
     mass_q = jnp.zeros((8, 128), F32)
     for b in range(8):
         line = qmb[b // 2, pl.ds(b % 2, 1), :]
@@ -133,10 +184,7 @@
     mass_t = jnp.concatenate([tmb[i] for i in range(NL)], axis=1)
 
     def dense(v):
-        out = jnp.zeros((8, 128), F32)
-        for c in range(TB // 128):
-            out = jnp.where(sub == c, v[:, c * 128:(c + 1) * 128], out)
-        return out
+        return jnp.concatenate([v[:, c * 128:(c + 1) * 128] for c in range(TB // 128)], axis=0)
 
     def undense(v):
         return jnp.concatenate([v[c:c + 1, :] for c in range(TB // 128)], axis=1)
@@ -145,7 +193,7 @@
         rsend[n] = value
         rbuf[n, mine] = value
 
-        @pl.loop(1, 2 * CHIPS)
+        @pl.loop(0, 2 * CHIPS - 1)
         def _(j):
             send(rsend.at[n], rbuf.at[n, mine], r_send.at[n], r_recv.at[n], group_peer(j))
 
@@ -157,7 +205,7 @@
         csend[n] = value
         cbuf[n, z] = value
 
-        @pl.loop(1, NZ)
+        @pl.loop(0, NZ - 1)
         def _(j):
             send(csend.at[n], cbuf.at[n, z], c_send.at[n], c_recv.at[n], z_peer(j))
 
@@ -168,14 +216,6 @@
     def lse(parts):
         top = jnp.max(parts, axis=0)
         return top + jnp.log2(jnp.sum(jnp.exp2(parts - top[None]), axis=0))
-
-    RB = 64
-    NB = QB // RB
-
-    def pick(out, block, values):
-        for g in range(RB // 8):
-            out = jnp.where(lane == block * (RB // 8) + g, values[g * 8:(g + 1) * 8, :], out)
-        return out
 
     def spread_rows(value):
         def body(b, v):
@@ -187,28 +227,9 @@
     def wide(r0, rows):
         return jnp.concatenate([cols[pl.ds(r0, rows), :]] * (TB // 128), axis=1)
 
-    zero = jnp.zeros((8, 128), F32)
-
-    scale = LOG2E / (EPSILON * math.sqrt(D))
-    tools = tblk[...].reshape(TB, D)
-    MB = 256
-
-    def products(i, carry):
-        a = qblk[pl.ds(i * (MB // QS), MB // QS)].reshape(MB, D)
-        s = lax.dot_general(a, tools, (((1,), (1,)), ((), ())), preferred_element_type=F32)
-        plan[pl.ds(pl.multiple_of(i * MB, MB), MB), :] = s * scale
-        return carry
-
-    lax.fori_loop(0, QB // MB, products, 0)
-
-    def first_rows(i, carry):
-        tops, sums = carry
-        s = plan[pl.ds(pl.multiple_of(i * RB, RB), RB), :]
-        top = jnp.max(s, axis=1, keepdims=True)
-        total = jnp.sum(jnp.exp2(s - top), axis=1, keepdims=True)
-        return pick(tops, i, top), pick(sums, i, total)
-
-    tops, sums = lax.fori_loop(0, NB, first_rows, (zero, zero))
+    (top_a, sum_a), (top_b, sum_b) = early, products(zl // 2)
+    tops = jnp.maximum(top_a, top_b)
+    sums = sum_a * jnp.exp2(top_a - tops) + sum_b * jnp.exp2(top_b - tops)
     gather_rows(0, tops + jnp.log2(sums))
     first_f = jnp.log2(mass_q) - lse(wait_rows(0))
 
@@ -289,7 +310,7 @@
         send(w.at[pl.ds(y_ * NX, NX), sib], wsib.at[pl.ds(y_ * NX, NX)], ws_send, ws_recv.at[h], device(x, y, z, sib))
     gather_rows(3, sums)
 
-    own, other = tools, tsib[...].reshape(TB, D)
+    own, other = tblk[...].reshape(TB, D), tsib[...].reshape(TB, D)
     for h in range(NY):
         y_ = (y + 1 + h) % NY
         a = w[pl.ds(y_ * NX, NX), core].reshape(NX * QS, TB)
@@ -312,7 +333,7 @@
     wait(qpb.at[pl.ds(0, NL - 1)], o_recv.at[0])
     wait(tpb.at[pl.ds(0, NY - 1)], o_recv.at[1])
     qp_ref[...] = qpb[...]
-    tp_ref[...] = jnp.concatenate([tpb[i] for i in range(NY)], axis=1)
+    tp_ref[...] = dense(jnp.concatenate([tpb[i] for i in range(NY)], axis=1))
 
     totals = jnp.sum(wait_rows(3), axis=0)
     spread_rows(totals)
@@ -325,7 +346,7 @@
     wait(qblk.at[pl.ds(0, CHIPS - 1)], q_send)
     wait(qblk.at[pl.ds(0, CHIPS)], q_fwd)
     for way in (0, 1):
-        wait(tblk.at[pl.ds(0, STEPS[way])], t_send.at[way])
+        wait(tblk.at[pl.ds(0, REACH[way])], t_send.at[way])
     wait(tblk, s_send)
     wait(wsib, ws_send)
     wait(qmb.at[pl.ds(0, NY - 1)], m_send.at[0])
@@ -347,24 +368,25 @@
         out_shape=(
             jax.ShapeDtypeStruct((QS, D), BF16),
             jax.ShapeDtypeStruct((NL, 2, 128), F32),
-            jax.ShapeDtypeStruct((1, TB), F32),
+            jax.ShapeDtypeStruct((TB // 128, 128), F32),
         ),
-        in_specs=[vmem] * 4,
+        in_specs=[pl.BlockSpec(memory_space=pltpu.HBM)] * 4,
         out_specs=(vmem,) * 3,
         scratch_shapes=[
             V((2 * CHIPS, QS, D), BF16), V((NZ, TS, D), BF16), V((NZ, TS, D), BF16), V((QB, TB), F32),
             V((CHIPS, 2, QS, TB), BF16), V((CHIPS, QS, TB), BF16), V((CHIPS, QS, D), F32), V((CHIPS, QS, D), F32),
             V((QB, 128), F32),
-            V((4, 8, 128), F32), V((4, 2 * CHIPS, 8, 128), F32), V((3, 8, 128), F32), V((3, NZ, 8, 128), F32),
+            V((NL, 2, 128), F32), V((TB // 128, 128), F32),
+            V((4, 8, 128), F32), V((4, 2 * CHIPS, 8, 128), F32), V((3, TB // 128, 128), F32), V((3, NZ, TB // 128, 128), F32),
             V((NY, 2, 128), F32), V((NY, 1, NH * TS), F32), V((NL, 1, NH * TS), F32),
             V((NY, 2, 128), F32), V((NL, 2, 128), F32), V((NL, 1, NH * TS), F32), V((NY, 1, NH * TS), F32),
-            dma, dma((CHIPS,)), dma, dma, dma((2,)), dma((2, NZ // 2)), dma, dma, dma, dma((NY,)),
+            dma((4,)), dma, dma((CHIPS,)), dma, dma, dma((2,)), dma((2, NZ // 2, 3)), dma, dma, dma, dma((NY,)),
             dma((2,)), dma((2,)), dma((4,)), dma((4,)), dma((3,)), dma((3,)), dma((2,)), dma((2,)), dma, dma,
         ],
         compiler_params=pltpu.CompilerParams(
-            collective_id=0, has_side_effects=True, vmem_limit_bytes=48 * 1024 * 1024
+            collective_id=0, has_side_effects=True, vmem_limit_bytes=60 * 1024 * 1024
         ),
-    )(queries, tools, query_mass.reshape(NL, 2, 128), tool_mass.reshape(1, TB))
+    )(queries, tools, query_mass.reshape(NL, 2, 128), tool_mass.reshape(TB // 128, 128))
     return mapped, qp.reshape(QB), tp.reshape(TB)
 
 

time: 135 us -> 114 us (0.84)
  Pallas kernels: 130 us -> 111 us
    pallas_call x1, Pallas kernels: 130 us -> 111 us  [local(): pl.pallas_call(kernel, out_shape=(jax.ShapeDtypeStruct((QS, D), BF16), ja...]
    unnamed x8 -> x7, local copies, waits for them, and re-layouts: 2.9 us -> 2.7 us
where the time goes in v2:
time: 114 us
  Pallas kernels  111 us (97%)
  local copies, waits for them, and re-layouts  2.7 us (2%)
    pallas_call x1, Pallas kernels, local(): pl.pallas_call(kernel, out_shape=(jax.ShapeDtypeStruct((QS, D), BF16), ja...  111 us
    unnamed x7, local copies, waits for them, and re-layouts  2.7 us

profile of v2, /device:TPU:1, one launch (start us, length us, event | category | flops | bytes accessed | tf_op | source)
XLA Modules:
  0.0 113.9 jit_solution(147363959381701613)
XLA Ops:
  0.6 110.6 %shard_map.67 = (bf16[32,768]{1,0:T(8,128)(2,1)}, f32[4,2,128]{2,1,0:T(2,128)}, f32[6,128]{1,0:T(8,128)}) custom-call(bf16[32,768]{1,0:T(8,128)(2,1)} %q_hbm.1, bf16[48,768]{1,0:T(8,128)(2,1)} %t_hbm.1, f32[4,2,128]{2,1,0:T(2,128)} %bitcast.4, f32[6,128]{1,0:T(8,128)} %bitcast.5), custom_call_target="tpu_custom_call" | custom-call | tf_op jit(solution)/shard_map/pallas_call | solution.py:366
  111.2 0.0 copy-start.1
  111.2 1.4 %copy.10 = bf16[32,768]{1,0:T(8,128)(2,1)} copy(bf16[32,768]{1,0:T(8,128)(2,1)} %get-tuple-element.12) | data formatting | bytes 98304
  112.6 0.0 copy-done.1
  112.6 0.0 copy-start
  112.6 0.6 copy.11
  113.2 0.1 copy-done
  113.3 0.6 copy.12
Async XLA Ops:
  111.2 1.4 %copy-start.1 = (f32[4,2,128]{2,1,0:T(2,128)S(1)}, f32[4,2,128]{2,1,0:T(2,128)}, u32[]{:S(2)}) copy-start(f32[4,2,128]{2,1,0:T(2,128)} %get-tuple-element.7) | copy-start | bytes 12292
  112.6 0.7 copy-start

commit v3 on v2

--- a/solution.py
+++ b/solution.py
@@ -1,3 +1,4 @@
+import functools
 import math
 
 import jax
@@ -24,10 +25,10 @@
 def kernel(
     q_hbm, t_hbm, qm_hbm, tm_hbm,
     map_ref, qp_ref, tp_ref,
-    qblk, tblk, tsib, plan, w, wsib, part, got, cols,
+    qblk, tblk, tsib, plan, w, wsib, part, got, half, last, cols,
     qm_ref, tm_ref, rsend, rbuf, csend, cbuf, qmb, tms, tmb, fout, qpb, gout, tpb,
     l_sem, q_send, q_recv, q_fwd, q_sib, t_send, t_recv, s_send, s_recv, ws_send, ws_recv,
-    m_send, m_recv, r_send, r_recv, c_send, c_recv, o_send, o_recv, p_send, p_recv,
+    m_send, m_recv, r_send, r_recv, c_send, c_recv, o_send, o_recv, p_send, p_recv, h_send, h_recv,
 ):
     row, col = lax.axis_index("row"), lax.axis_index("col")
     y, zh = row // NH, row % NH
@@ -49,9 +50,6 @@
         x_ = (x + far((j // 2) % NX, NX)) % NX
         return device(x_, y_, z, (core + 1 + j) % 2)
 
-    def chip_peer(j):
-        return (x + j % NX) % NX, (y + j // NX) % NY
-
     def z_peer(j):
         return device(x, y, (z + far(j, NZ)) % NZ, core)
 
@@ -68,9 +66,14 @@
         peer = device(x, y, (z + near) % NZ, core)
         pl.semaphore_signal(barrier, inc=1, device_id=peer, device_id_type=MESH)
 
-    @pl.loop(0, 2 * CHIPS - 1)
-    def _(j):
-        pl.semaphore_signal(barrier, inc=1, device_id=group_peer(j), device_id_type=MESH)
+    hops = {0: 0, 1: 1, 2: 2, 3: 1}
+    shifts = [(a, b) for a in (2, 1, 3, 0) for b in (2, 1, 3, 0) if (a, b) != (0, 0)]
+    near_chips = [s for s in shifts if hops[s[0]] + hops[s[1]] <= 2]
+    far_chips = [s for s in shifts if s not in near_chips]
+    for a, b in near_chips + [(0, 0)]:
+        for core_ in (sib, core) if (a, b) != (0, 0) else (sib,):
+            peer = device((x + a) % NX, (y + b) % NY, z, core_)
+            pl.semaphore_signal(barrier, inc=1, device_id=peer, device_id_type=MESH)
 
     loads = [
         pltpu.make_async_copy(t_hbm, tblk.at[slot], l_sem.at[0]),
@@ -85,7 +88,7 @@
     tms_all = jnp.concatenate([tm_ref[c:c + 1, :] for c in range(TB // 128)], axis=1)
     for i in range(NY):
         tms[i] = tms_all[:, i * NH * TS:(i + 1) * NH * TS]
-    pl.semaphore_wait(barrier, 2 * CHIPS - 1 + 4)
+    pl.semaphore_wait(barrier, 2 * len(near_chips) + 1 + 4)
 
     lane = lax.broadcasted_iota(jnp.int32, (8, 128), 1)
     zero = jnp.zeros((8, 128), F32)
@@ -124,47 +127,59 @@
     def t_piece(source, p):
         return tblk.at[t_slot(source), pl.ds(p * PIECE, PIECE)]
 
-    REACH = (NZ // 2, NZ // 2 - 1)
+    def reach(way, p):
+        return NZ // 2 if (way == 0) == (p < 2) else NZ // 2 - 1
 
     def t_source(way, dist):
         return (z + NZ - dist) % NZ if way == 0 else (z + dist) % NZ
 
+    ONWARD = {0: (2, 1), 2: (4, 3), 4: (5,), 5: (6,), 6: (7,), 7: (8,)}
+
     def t_forward(way, dist, p):
         piece = t_piece(t_source(way, dist), p)
-        for hop in (2, 1):
-            if dist % 2 == 0 and dist + hop <= REACH[way]:
-                to = device(x, y, t_source(way, NZ - hop), core)
-                send(piece, piece, t_send.at[way], t_recv.at[way, dist + hop - 1, p], to)
+        for there in ONWARD.get(dist, ()):
+            if there <= reach(way, p):
+                to = device(x, y, t_source(way, NZ + dist - there), core)
+                send(piece, piece, t_send.at[way], t_recv.at[way, there - 1, p], to)
 
     for p in range(PIECES):
         for way in (0, 1):
             t_forward(way, 0, p)
 
-    @pl.loop(1, CHIPS)
-    def _(j):
-        x_, y_ = chip_peer(j)
-        send(qblk.at[mine], qblk.at[mine], q_send, q_recv.at[chip], device(x_, y_, z, core))
-
+    def q_give(a, b):
+        to = device((x + a) % NX, (y + b) % NY, z, core)
+        send(qblk.at[mine], qblk.at[mine], q_send, q_recv.at[chip], to)
+
+    def q_take(a, b):
+        chip_ = ((y + b) % NY) * NX + (x + a) % NX
+        s = chip_ * 2 + core
+        wait(qblk.at[s], q_recv.at[chip_])
+        send(qblk.at[s], qblk.at[s], q_fwd, q_sib, device(x, y, z, sib))
+
+    for a, b in near_chips:
+        q_give(a, b)
+    corners = [(1, 1), (3, 1), (1, 3)]
+    others = [s for s in near_chips if s not in corners] + far_chips
     send(qblk.at[mine], qblk.at[mine], q_fwd, q_sib, device(x, y, z, sib))
     for j in range(1, NY):
         send(qm_ref.at[zl], qmb.at[y], m_send.at[0], m_recv.at[0], device(x, (y + j) % NY, z, core))
     qmb[y] = qm_ref[zl]
     tmb[zl] = tms[y]
 
-    for step, dist in enumerate((2, 1, 4, 3, 6, 5, 7, 8)):
+    for step, dist in enumerate((2, 1, 4, 3, 5, 6, 7, 8)):
         for p in range(PIECES):
             for way in (0, 1):
-                if dist <= REACH[way]:
+                if dist <= reach(way, p):
                     wait(t_piece(t_source(way, dist), p), t_recv.at[way, dist - 1, p])
                     t_forward(way, dist, p)
-        for j in range(1 + 3 * (step - 2), min(4 + 3 * (step - 2), CHIPS)):
-            if j < 1:
-                continue
-            x_, y_ = (x + NX - j % NX) % NX, (y + NY - j // NX) % NY
-            chip_ = y_ * NX + x_
-            s = chip_ * 2 + core
-            wait(qblk.at[s], q_recv.at[chip_])
-            send(qblk.at[s], qblk.at[s], q_fwd, q_sib, device(x, y, z, sib))
+        if step == 1:
+            for a, b in corners:
+                q_take(a, b)
+            for a, b in far_chips:
+                q_give(a, b)
+        if 3 <= step < 7:
+            for a, b in others[3 * (step - 3):3 * (step - 2)]:
+                q_take(a, b)
         if step == NL - 1:
             for j in range(1, NL):
                 send(tms.at[y], tmb.at[zl], m_send.at[1], m_recv.at[1], device(x, y, zh * NL + (zl + j) % NL, core))
@@ -218,11 +233,8 @@
         return top + jnp.log2(jnp.sum(jnp.exp2(parts - top[None]), axis=0))
 
     def spread_rows(value):
-        def body(b, v):
-            for k in range(16):
-                cols[pl.ds(pl.multiple_of(b * 128 + k * 8, 8), 8), :] = jnp.broadcast_to(v[:, k:k + 1], (8, 128))
-            return pltpu.roll(v, 112, 1)
-        lax.fori_loop(0, 8, body, value)
+        for k in range(QB // 8):
+            cols[k * 8:k * 8 + 8, :] = jnp.broadcast_to(value[:, k:k + 1], (8, 128))
 
     def wide(r0, rows):
         return jnp.concatenate([cols[pl.ds(r0, rows), :]] * (TB // 128), axis=1)
@@ -295,8 +307,8 @@
 
     PB = 2 * QS
 
-    def weights(i, sums):
-        c = ((y + 1 + i // NX) % NY) * NX + i % NX
+    def weights(y_, i, sums):
+        c = y_ * NX + i
         r0 = pl.multiple_of(c * PB, PB)
         e = (plan[pl.ds(r0, PB), :] * wide(r0, PB) * v).astype(BF16)
         w[c] = e.reshape(2, QS, TB)
@@ -305,24 +317,46 @@
     wait(tsib, s_recv)
     sums = zero
     for h in range(NY):
-        sums = lax.fori_loop(h * NX, (h + 1) * NX, weights, sums)
-        y_ = (y + 1 + h) % NY
+        y_ = (y + (2, 1, 3, 0)[h]) % NY
+        sums = lax.fori_loop(0, NX, functools.partial(weights, y_), sums)
         send(w.at[pl.ds(y_ * NX, NX), sib], wsib.at[pl.ds(y_ * NX, NX)], ws_send, ws_recv.at[h], device(x, y, z, sib))
     gather_rows(3, sums)
 
     own, other = tblk[...].reshape(TB, D), tsib[...].reshape(TB, D)
-    for h in range(NY):
-        y_ = (y + 1 + h) % NY
+    HD = D // 2
+    for h, dy in enumerate((2, 1, 3, 0)):
+        y_ = (y + dy) % NY
         a = w[pl.ds(y_ * NX, NX), core].reshape(NX * QS, TB)
         p = jnp.dot(a, own, preferred_element_type=F32)
         wait(wsib.at[pl.ds(y_ * NX, NX)], ws_recv.at[h])
         b = wsib[pl.ds(y_ * NX, NX)].reshape(NX * QS, TB)
         p = p + jnp.dot(b, other, preferred_element_type=F32)
-        part[pl.ds(y_ * NX, NX)] = p.reshape(NX, QS, D)
-        for j in range(NX):
-            x_ = (x + 1 + j) % NX
-            if h < NY - 1 or j < NX - 1:
-                send(part.at[y_ * NX + x_], got.at[chip], p_send, p_recv, device(x_, y_, z, core))
+        for f in (0, 1):
+            part[f, pl.ds(y_ * NX, NX)] = p[:, f * HD:(f + 1) * HD].reshape(NX, QS, HD)
+        for dx in (2, 1, 3, 0):
+            x_ = (x + dx) % NX
+            if dx:
+                send(part.at[0, y_ * NX + x_], got.at[0, y_, x], p_send.at[0], p_recv.at[0, y_], device(x_, y, z, core))
+            else:
+                got[0, y_, x] = part[0, y_ * NX + x]
+            if dy:
+                send(part.at[1, y_ * NX + x_], got.at[1, x_, y], p_send.at[1], p_recv.at[1, x_], device(x, y_, z, core))
+            else:
+                got[1, x_, y] = part[1, y * NX + x_]
+
+    def second(f, d):
+        at = (y + d) % NY if f == 0 else (x + d) % NX
+        wait(got.at[f, at, pl.ds(0, 3)], p_recv.at[f, at])
+        total_ = jnp.sum(got[f, at], axis=0)
+        if d:
+            half[f, at] = total_
+            to = device(x, at, z, core) if f == 0 else device(at, y, z, core)
+            send(half.at[f, at], last.at[f, y if f == 0 else x], h_send.at[f], h_recv.at[f], to)
+        else:
+            last[f, at] = total_
+
+    for f, d in ((0, 2), (0, 1), (1, 2), (0, 3), (1, 1), (1, 3), (0, 0), (1, 0)):
+        second(f, d)
 
     g = (first_g + jnp.log2(v)) * POT
     for i in range(NL):
@@ -338,15 +372,16 @@
     totals = jnp.sum(wait_rows(3), axis=0)
     spread_rows(totals)
     total = cols[pl.ds(pl.multiple_of(mine * QS, QS), QS), :]
-    got[chip] = part[chip]
-    wait(got.at[pl.ds(0, CHIPS - 1)], p_recv)
-    full = jnp.sum(got[...], axis=0)
+    for f in (0, 1):
+        wait(last.at[f, pl.ds(0, 3)], h_recv.at[f])
+    full = jnp.concatenate([jnp.sum(last[f], axis=0) for f in (0, 1)], axis=1)
     map_ref[...] = (full / jnp.concatenate([total] * (D // 128), axis=1)).astype(BF16)
 
     wait(qblk.at[pl.ds(0, CHIPS - 1)], q_send)
     wait(qblk.at[pl.ds(0, CHIPS)], q_fwd)
     for way in (0, 1):
-        wait(tblk.at[pl.ds(0, REACH[way])], t_send.at[way])
+        for p in range(PIECES):
+            wait(tblk.at[pl.ds(0, reach(way, p)), pl.ds(p * PIECE, PIECE)], t_send.at[way])
     wait(tblk, s_send)
     wait(wsib, ws_send)
     wait(qmb.at[pl.ds(0, NY - 1)], m_send.at[0])
@@ -357,7 +392,9 @@
         wait(rbuf.at[n, pl.ds(0, 2 * CHIPS - 1)], r_send.at[n])
     for n in range(3):
         wait(cbuf.at[n, pl.ds(0, NZ - 1)], c_send.at[n])
-    wait(got.at[pl.ds(0, CHIPS - 1)], p_send)
+    for f in (0, 1):
+        wait(part.at[f, pl.ds(0, 3 * NX)], p_send.at[f])
+        wait(last.at[f, pl.ds(0, 3)], h_send.at[f])
 
 
 def local(queries, tools, query_mass, tool_mass):
@@ -374,14 +411,17 @@
         out_specs=(vmem,) * 3,
         scratch_shapes=[
             V((2 * CHIPS, QS, D), BF16), V((NZ, TS, D), BF16), V((NZ, TS, D), BF16), V((QB, TB), F32),
-            V((CHIPS, 2, QS, TB), BF16), V((CHIPS, QS, TB), BF16), V((CHIPS, QS, D), F32), V((CHIPS, QS, D), F32),
+            V((CHIPS, 2, QS, TB), BF16), V((CHIPS, QS, TB), BF16),
+            V((2, CHIPS, QS, D // 2), F32), V((2, 4, 4, QS, D // 2), F32),
+            V((2, 4, QS, D // 2), F32), V((2, 4, QS, D // 2), F32),
             V((QB, 128), F32),
             V((NL, 2, 128), F32), V((TB // 128, 128), F32),
             V((4, 8, 128), F32), V((4, 2 * CHIPS, 8, 128), F32), V((3, TB // 128, 128), F32), V((3, NZ, TB // 128, 128), F32),
             V((NY, 2, 128), F32), V((NY, 1, NH * TS), F32), V((NL, 1, NH * TS), F32),
             V((NY, 2, 128), F32), V((NL, 2, 128), F32), V((NL, 1, NH * TS), F32), V((NY, 1, NH * TS), F32),
             dma((4,)), dma, dma((CHIPS,)), dma, dma, dma((2,)), dma((2, NZ // 2, 3)), dma, dma, dma, dma((NY,)),
-            dma((2,)), dma((2,)), dma((4,)), dma((4,)), dma((3,)), dma((3,)), dma((2,)), dma((2,)), dma, dma,
+            dma((2,)), dma((2,)), dma((4,)), dma((4,)), dma((3,)), dma((3,)), dma((2,)), dma((2,)),
+            dma((2,)), dma((2, 4)), dma((2,)), dma((2,)),
         ],
         compiler_params=pltpu.CompilerParams(
             collective_id=0, has_side_effects=True, vmem_limit_bytes=60 * 1024 * 1024

time: 114 us -> 108 us (0.947)
  Pallas kernels: 111 us -> 104 us
    pallas_call x1, Pallas kernels: 111 us -> 104 us  [local(): pl.pallas_call(kernel, out_shape=(jax.ShapeDtypeStruct((QS, D), BF16), ja...]
where the time goes in v3:
time: 108 us; the launch traced here: 107 us
  Pallas kernels  104 us (96%)
  local copies, waits for them, and re-layouts  2.7 us (2%)
    pallas_call x1, Pallas kernels, local(): pl.pallas_call(kernel, out_shape=(jax.ShapeDtypeStruct((QS, D), BF16), ja...  104 us
    unnamed x7, local copies, waits for them, and re-layouts  2.7 us

profile of v3, /device:TPU:1, one launch (start us, length us, event | category | flops | bytes accessed | tf_op | source)
XLA Modules:
  0.0 107.4 jit_solution(5255972757371010111)
XLA Ops:
  0.6 104.0 %shard_map.67 = (bf16[32,768]{1,0:T(8,128)(2,1)}, f32[4,2,128]{2,1,0:T(2,128)}, f32[6,128]{1,0:T(8,128)}) custom-call(bf16[32,768]{1,0:T(8,128)(2,1)} %q_hbm.1, bf16[48,768]{1,0:T(8,128)(2,1)} %t_hbm.1, f32[4,2,128]{2,1,0:T(2,128)} %bitcast.4, f32[6,128]{1,0:T(8,128)} %bitcast.5), custom_call_target="tpu_custom_call" | custom-call | tf_op jit(solution)/shard_map/pallas_call | solution.py:403
  104.7 0.0 copy-start.1
  104.7 1.4 %copy.10 = bf16[32,768]{1,0:T(8,128)(2,1)} copy(bf16[32,768]{1,0:T(8,128)(2,1)} %get-tuple-element.12) | data formatting | bytes 98304
  106.1 0.0 copy-done.1
  106.1 0.0 copy-start
  106.1 0.6 copy.11
  106.7 0.1 copy-done
  106.8 0.6 copy.12
Async XLA Ops:
  104.7 1.4 %copy-start.1 = (f32[4,2,128]{2,1,0:T(2,128)S(1)}, f32[4,2,128]{2,1,0:T(2,128)}, u32[]{:S(2)}) copy-start(f32[4,2,128]{2,1,0:T(2,128)} %get-tuple-element.7) | copy-start | bytes 12292
  106.1 0.7 copy-start

commit v4 on v3

--- a/solution.py
+++ b/solution.py
@@ -42,16 +42,14 @@
     def device(x_, y_, z_, core_):
         return (y_ * NH + z_ // NL, ((z_ % NL) * NX + x_) * 2 + core_)
 
-    def far(j, n):
-        return (n // 2 + ((j + 1) // 2) * (1 - 2 * (j % 2)) + n) % n
-
-    def group_peer(j):
-        y_ = (y + far(j // (2 * NX), NY)) % NY
-        x_ = (x + far((j // 2) % NX, NX)) % NX
-        return device(x_, y_, z, (core + 1 + j) % 2)
-
-    def z_peer(j):
-        return device(x, y, (z + far(j, NZ)) % NZ, core)
+    rows_at = [((y + b) % NY) * NH + zh for b in range(NY)]
+    cols_at = [(zl * NX + (x + a) % NX) * 2 for a in range(NX)]
+    plane = [
+        (rows_at[b], cols_at[a] + core_)
+        for b in (2, 1, 3, 0) for a in (2, 1, 3, 0) for core_ in (sib, core)
+    ][:-1]
+    others_z = [(z + d) % NZ for d in (8, 7, 9, 6, 10, 5, 11, 4, 12, 3, 13, 2, 14, 1, 15)]
+    column = [device(x, y, z_, core) for z_ in others_z]
 
     def send(src, dst, s_sem, r_sem, dev):
         pltpu.make_async_remote_copy(
@@ -133,7 +131,7 @@
     def t_source(way, dist):
         return (z + NZ - dist) % NZ if way == 0 else (z + dist) % NZ
 
-    ONWARD = {0: (2, 1), 2: (4, 3), 4: (5,), 5: (6,), 6: (7,), 7: (8,)}
+    ONWARD = {0: (2, 1), 2: (4, 3), 4: (6, 5), 6: (7,), 7: (8,)}
 
     def t_forward(way, dist, p):
         piece = t_piece(t_source(way, dist), p)
@@ -166,7 +164,7 @@
     qmb[y] = qm_ref[zl]
     tmb[zl] = tms[y]
 
-    for step, dist in enumerate((2, 1, 4, 3, 5, 6, 7, 8)):
+    for step, dist in enumerate((2, 1, 4, 3, 6, 5, 7, 8)):
         for p in range(PIECES):
             for way in (0, 1):
                 if dist <= reach(way, p):
@@ -186,6 +184,50 @@
         if step == NZ // 2 - 2:
             wait(qblk.at[pl.ds(0, CHIPS)], q_sib)
             early = products(1 - zl // 2)
+
+    def dense(v):
+        return jnp.concatenate([v[:, c * 128:(c + 1) * 128] for c in range(TB // 128)], axis=0)
+
+    def undense(v):
+        return jnp.concatenate([v[c:c + 1, :] for c in range(TB // 128)], axis=1)
+
+    def gather_rows(n, value):
+        rsend[n] = value
+        rbuf[n, mine] = value
+
+        for peer in plane:
+            send(rsend.at[n], rbuf.at[n, mine], r_send.at[n], r_recv.at[n], peer)
+
+    def wait_rows(n):
+        wait(rbuf.at[n, pl.ds(0, 2 * CHIPS - 1)], r_recv.at[n])
+        return rbuf[n]
+
+    def gather_cols(n, value):
+        csend[n] = value
+        cbuf[n, z] = value
+
+        for peer in column:
+            send(csend.at[n], cbuf.at[n, z], c_send.at[n], c_recv.at[n], peer)
+
+    def wait_cols(n):
+        wait(cbuf.at[n, pl.ds(0, NZ - 1)], c_recv.at[n])
+        return cbuf[n]
+
+    def lse(parts):
+        top = jnp.max(parts, axis=0)
+        return top + jnp.log2(jnp.sum(jnp.exp2(parts - top[None]), axis=0))
+
+    def spread_rows(value):
+        for k in range(QB // 8):
+            cols[k * 8:k * 8 + 8, :] = jnp.broadcast_to(value[:, k:k + 1], (8, 128))
+
+    def wide(r0, rows):
+        return jnp.concatenate([cols[pl.ds(r0, rows), :]] * (TB // 128), axis=1)
+
+    (top_a, sum_a), (top_b, sum_b) = early, products(zl // 2)
+    tops = jnp.maximum(top_a, top_b)
+    sums = sum_a * jnp.exp2(top_a - tops) + sum_b * jnp.exp2(top_b - tops)
+    gather_rows(0, tops + jnp.log2(sums))
     send(tblk, tsib, s_send, s_recv, device(x, y, z, sib))
 
     wait(qmb.at[pl.ds(0, NY - 1)], m_recv.at[0])
@@ -198,51 +240,6 @@
             mass_q = jnp.where(lane == b * 16 + k, spread[k * 8:k * 8 + 8, :], mass_q)
     mass_t = jnp.concatenate([tmb[i] for i in range(NL)], axis=1)
 
-    def dense(v):
-        return jnp.concatenate([v[:, c * 128:(c + 1) * 128] for c in range(TB // 128)], axis=0)
-
-    def undense(v):
-        return jnp.concatenate([v[c:c + 1, :] for c in range(TB // 128)], axis=1)
-
-    def gather_rows(n, value):
-        rsend[n] = value
-        rbuf[n, mine] = value
-
-        @pl.loop(0, 2 * CHIPS - 1)
-        def _(j):
-            send(rsend.at[n], rbuf.at[n, mine], r_send.at[n], r_recv.at[n], group_peer(j))
-
-    def wait_rows(n):
-        wait(rbuf.at[n, pl.ds(0, 2 * CHIPS - 1)], r_recv.at[n])
-        return rbuf[n]
-
-    def gather_cols(n, value):
-        csend[n] = value
-        cbuf[n, z] = value
-
-        @pl.loop(0, NZ - 1)
-        def _(j):
-            send(csend.at[n], cbuf.at[n, z], c_send.at[n], c_recv.at[n], z_peer(j))
-
-    def wait_cols(n):
-        wait(cbuf.at[n, pl.ds(0, NZ - 1)], c_recv.at[n])
-        return cbuf[n]
-
-    def lse(parts):
-        top = jnp.max(parts, axis=0)
-        return top + jnp.log2(jnp.sum(jnp.exp2(parts - top[None]), axis=0))
-
-    def spread_rows(value):
-        for k in range(QB // 8):
-            cols[k * 8:k * 8 + 8, :] = jnp.broadcast_to(value[:, k:k + 1], (8, 128))
-
-    def wide(r0, rows):
-        return jnp.concatenate([cols[pl.ds(r0, rows), :]] * (TB // 128), axis=1)
-
-    (top_a, sum_a), (top_b, sum_b) = early, products(zl // 2)
-    tops = jnp.maximum(top_a, top_b)
-    sums = sum_a * jnp.exp2(top_a - tops) + sum_b * jnp.exp2(top_b - tops)
-    gather_rows(0, tops + jnp.log2(sums))
     first_f = jnp.log2(mass_q) - lse(wait_rows(0))
 
     spread_rows(first_f)
@@ -320,7 +317,6 @@
         y_ = (y + (2, 1, 3, 0)[h]) % NY
         sums = lax.fori_loop(0, NX, functools.partial(weights, y_), sums)
         send(w.at[pl.ds(y_ * NX, NX), sib], wsib.at[pl.ds(y_ * NX, NX)], ws_send, ws_recv.at[h], device(x, y, z, sib))
-    gather_rows(3, sums)
 
     own, other = tblk[...].reshape(TB, D), tsib[...].reshape(TB, D)
     HD = D // 2
@@ -343,6 +339,8 @@
                 send(part.at[1, y_ * NX + x_], got.at[1, x_, y], p_send.at[1], p_recv.at[1, x_], device(x, y_, z, core))
             else:
                 got[1, x_, y] = part[1, y * NX + x_]
+
+    gather_rows(3, sums)
 
     def second(f, d):
         at = (y + d) % NY if f == 0 else (x + d) % NX

time: 108 us -> 105 us (0.972)
  Pallas kernels: 104 us -> 101 us
    pallas_call x1, Pallas kernels: 104 us -> 101 us  [local(): pl.pallas_call(kernel, out_shape=(jax.ShapeDtypeStruct((QS, D), BF16), ja...]
where the time goes in v4:
time: 105 us
  Pallas kernels  101 us (96%)
  local copies, waits for them, and re-layouts  2.7 us (3%)
    pallas_call x1, Pallas kernels, local(): pl.pallas_call(kernel, out_shape=(jax.ShapeDtypeStruct((QS, D), BF16), ja...  101 us
    unnamed x7, local copies, waits for them, and re-layouts  2.7 us

profile of v4, /device:TPU:1, one launch (start us, length us, event | category | flops | bytes accessed | tf_op | source)
XLA Modules:
  0.0 104.6 jit_solution(1554057386469368952)
XLA Ops:
  0.6 101.3 %shard_map.67 = (bf16[32,768]{1,0:T(8,128)(2,1)}, f32[4,2,128]{2,1,0:T(2,128)}, f32[6,128]{1,0:T(8,128)}) custom-call(bf16[32,768]{1,0:T(8,128)(2,1)} %q_hbm.1, bf16[48,768]{1,0:T(8,128)(2,1)} %t_hbm.1, f32[4,2,128]{2,1,0:T(2,128)} %bitcast.4, f32[6,128]{1,0:T(8,128)} %bitcast.5), custom_call_target="tpu_custom_call" | custom-call | tf_op jit(solution)/shard_map/pallas_call | solution.py:401
  101.9 0.0 copy-start.1
  101.9 1.4 %copy.10 = bf16[32,768]{1,0:T(8,128)(2,1)} copy(bf16[32,768]{1,0:T(8,128)(2,1)} %get-tuple-element.12) | data formatting | bytes 98304
  103.4 0.0 copy-done.1
  103.4 0.0 copy-start
  103.4 0.6 copy.11
  104.0 0.1 copy-done
  104.0 0.6 copy.12
Async XLA Ops:
  101.9 1.4 %copy-start.1 = (f32[4,2,128]{2,1,0:T(2,128)S(1)}, f32[4,2,128]{2,1,0:T(2,128)}, u32[]{:S(2)}) copy-start(f32[4,2,128]{2,1,0:T(2,128)} %get-tuple-element.7) | copy-start | bytes 12292
  103.4 0.7 copy-start

commit v5 on v4

--- a/solution.py
+++ b/solution.py
@@ -115,7 +115,7 @@
             total = jnp.sum(jnp.exp2(s - top), axis=1, keepdims=True)
             return pick(tops, i, top), pick(sums, i, total)
 
-        return lax.fori_loop(0, QB // MB, body, (zero, zero))
+        return lax.fori_loop(0, QB // MB, body, (zero, zero), unroll=4)
 
     def t_slot(z_):
         return (z_ % NL) * NH + z_ // NL
@@ -250,14 +250,14 @@
         plan[pl.ds(r0, RB), :] = s
         return jnp.maximum(top, jnp.max(s.reshape(RB // 8, 8, TB), axis=0))
 
-    top8 = lax.fori_loop(0, NB, col_max, jnp.full((8, TB), -jnp.inf, F32))
+    top8 = lax.fori_loop(0, NB, col_max, jnp.full((8, TB), -jnp.inf, F32), unroll=4)
     top = jnp.max(top8, axis=0, keepdims=True)
 
     def col_sum(i, acc):
         s = plan[pl.ds(pl.multiple_of(i * RB, RB), RB), :]
         return acc + jnp.sum(jnp.exp2(s - top).reshape(RB // 8, 8, TB), axis=0)
 
-    acc = lax.fori_loop(0, NB, col_sum, jnp.zeros((8, TB), F32))
+    acc = lax.fori_loop(0, NB, col_sum, jnp.zeros((8, TB), F32), unroll=4)
     gather_cols(0, dense(top + jnp.log2(jnp.sum(acc, axis=0, keepdims=True))))
     first_g = jnp.log2(mass_t) - undense(lse(wait_cols(0)))
 
@@ -271,17 +271,17 @@
         def body(i, sums):
             e = plan[pl.ds(pl.multiple_of(i * RB, RB), RB), :] * v
             return pick(sums, i, jnp.sum(e, axis=1, keepdims=True))
-        return lax.fori_loop(0, NB, body, zero)
+        return lax.fori_loop(0, NB, body, zero, unroll=4)
 
     def later_cols():
         def body(i, acc):
             r0 = pl.multiple_of(i * RB, RB)
             e = plan[pl.ds(r0, RB), :] * wide(r0, RB)
             return acc + jnp.sum(e.reshape(RB // 8, 8, TB), axis=0)
-        acc = lax.fori_loop(0, NB, body, jnp.zeros((8, TB), F32))
+        acc = lax.fori_loop(0, NB, body, jnp.zeros((8, TB), F32), unroll=4)
         return dense(jnp.sum(acc, axis=0, keepdims=True))
 
-    gather_rows(1, lax.fori_loop(0, NB, second_rows, zero))
+    gather_rows(1, lax.fori_loop(0, NB, second_rows, zero, unroll=4))
     u = mass_q / jnp.sum(wait_rows(1), axis=0)
     spread_rows(u)
     gather_cols(1, later_cols())
@@ -315,7 +315,7 @@
     sums = zero
     for h in range(NY):
         y_ = (y + (2, 1, 3, 0)[h]) % NY
-        sums = lax.fori_loop(0, NX, functools.partial(weights, y_), sums)
+        sums = lax.fori_loop(0, NX, functools.partial(weights, y_), sums, unroll=2)
         send(w.at[pl.ds(y_ * NX, NX), sib], wsib.at[pl.ds(y_ * NX, NX)], ws_send, ws_recv.at[h], device(x, y, z, sib))
 
     own, other = tblk[...].reshape(TB, D), tsib[...].reshape(TB, D)

time: 105 us -> 101 us (0.962)
  Pallas kernels: 101 us -> 97.2 us
    pallas_call x1, Pallas kernels: 101 us -> 97.2 us  [local(): pl.pallas_call(kernel, out_shape=(jax.ShapeDtypeStruct((QS, D), BF16), ja...]
where the time goes in v5:
time: 101 us
  Pallas kernels  97.2 us (96%)
  local copies, waits for them, and re-layouts  2.7 us (3%)
    pallas_call x1, Pallas kernels, local(): pl.pallas_call(kernel, out_shape=(jax.ShapeDtypeStruct((QS, D), BF16), ja...  97.2 us
    unnamed x7, local copies, waits for them, and re-layouts  2.7 us

profile of v5, /device:TPU:1, one launch (start us, length us, event | category | flops | bytes accessed | tf_op | source)
XLA Modules:
  0.0 100.6 jit_solution(2130363513528581105)
XLA Ops:
  0.6 97.2 %shard_map.67 = (bf16[32,768]{1,0:T(8,128)(2,1)}, f32[4,2,128]{2,1,0:T(2,128)}, f32[6,128]{1,0:T(8,128)}) custom-call(bf16[32,768]{1,0:T(8,128)(2,1)} %q_hbm.1, bf16[48,768]{1,0:T(8,128)(2,1)} %t_hbm.1, f32[4,2,128]{2,1,0:T(2,128)} %bitcast.4, f32[6,128]{1,0:T(8,128)} %bitcast.5), custom_call_target="tpu_custom_call" | custom-call | tf_op jit(solution)/shard_map/pallas_call | solution.py:401
  97.9 0.0 copy-start.1
  97.9 1.4 %copy.10 = bf16[32,768]{1,0:T(8,128)(2,1)} copy(bf16[32,768]{1,0:T(8,128)(2,1)} %get-tuple-element.12) | data formatting | bytes 98304
  99.3 0.0 copy-done.1
  99.3 0.0 copy-start
  99.3 0.6 copy.11
  99.9 0.1 copy-done
  100.0 0.6 copy.12
Async XLA Ops:
  97.9 1.4 %copy-start.1 = (f32[4,2,128]{2,1,0:T(2,128)S(1)}, f32[4,2,128]{2,1,0:T(2,128)}, u32[]{:S(2)}) copy-start(f32[4,2,128]{2,1,0:T(2,128)} %get-tuple-element.7) | copy-start | bytes 12292
  99.3 0.7 copy-start

commit v6 on v5

--- a/solution.py
+++ b/solution.py
@@ -175,8 +175,8 @@
                 q_take(a, b)
             for a, b in far_chips:
                 q_give(a, b)
-        if 3 <= step < 7:
-            for a, b in others[3 * (step - 3):3 * (step - 2)]:
+        if 4 <= step < 7:
+            for a, b in others[4 * (step - 4):4 * (step - 3)]:
                 q_take(a, b)
         if step == NL - 1:
             for j in range(1, NL):

time: 101 us -> 101 us (level)
  no operation moved by 1% of the time
where the time goes in v6:
time: 101 us
  Pallas kernels  97.2 us (96%)
  local copies, waits for them, and re-layouts  2.7 us (3%)
    pallas_call x1, Pallas kernels, local(): pl.pallas_call(kernel, out_shape=(jax.ShapeDtypeStruct((QS, D), BF16), ja...  97.2 us
    unnamed x7, local copies, waits for them, and re-layouts  2.7 us

profile of v6, /device:TPU:1, one launch (start us, length us, event | category | flops | bytes accessed | tf_op | source)
XLA Modules:
  0.0 100.6 jit_solution(5083985516673834995)
XLA Ops:
  0.6 97.2 %shard_map.67 = (bf16[32,768]{1,0:T(8,128)(2,1)}, f32[4,2,128]{2,1,0:T(2,128)}, f32[6,128]{1,0:T(8,128)}) custom-call(bf16[32,768]{1,0:T(8,128)(2,1)} %q_hbm.1, bf16[48,768]{1,0:T(8,128)(2,1)} %t_hbm.1, f32[4,2,128]{2,1,0:T(2,128)} %bitcast.4, f32[6,128]{1,0:T(8,128)} %bitcast.5), custom_call_target="tpu_custom_call" | custom-call | tf_op jit(solution)/shard_map/pallas_call | solution.py:401
  97.9 0.0 copy-start.1
  97.9 1.4 %copy.10 = bf16[32,768]{1,0:T(8,128)(2,1)} copy(bf16[32,768]{1,0:T(8,128)(2,1)} %get-tuple-element.12) | data formatting | bytes 98304
  99.3 0.0 copy-done.1
  99.3 0.0 copy-start
  99.3 0.6 copy.11
  99.9 0.1 copy-done
  100.0 0.6 copy.12
Async XLA Ops:
  97.9 1.4 %copy-start.1 = (f32[4,2,128]{2,1,0:T(2,128)S(1)}, f32[4,2,128]{2,1,0:T(2,128)}, u32[]{:S(2)}) copy-start(f32[4,2,128]{2,1,0:T(2,128)} %get-tuple-element.7) | copy-start | bytes 12292
  99.3 0.7 copy-start
